TPU v7x, 32 devices: a whole 2x2x4 slice. The times are simulated.
32 devices in a mesh: groups: 2 (over x), tile: 16 (over z, y, core).
Axes of the slice: x: 2, y: 2, z: 4, core: 2. Of those that a mesh axis runs over, the one named last changes fastest.
Arguments:
- features: bfloat16 [8, 384, 16, 8, 16], P('groups', None, 'tile'), parts along dimension 0, may hold values from -6 to 6
- cache_first: bfloat16 [4, 384, 16, 8, 16], P('groups', None, 'tile'), parts along dimension 0, may hold values from -6 to 6
- cache_second: bfloat16 [4, 192, 16, 16, 32], P('groups', None, 'tile'), parts along dimension 0, may hold values from -6 to 6
- cache_third: bfloat16 [4, 96, 16, 32, 64], P('groups', None, 'tile'), parts along dimension 0, may hold values from -6 to 6
- weight_first: bfloat16 [3, 3, 3, 192, 384], replicated, may hold values from -0.0625 to 0.0625
- weight_second: bfloat16 [3, 3, 3, 96, 192], replicated, may hold values from -0.078125 to 0.078125
- weight_third: bfloat16 [3, 3, 3, 3, 96], replicated, may hold values from -0.125 to 0.125
- gain_first: float32 [384], replicated, may hold values from 0.1 to 1.9
- gain_second: float32 [192], replicated, may hold values from 0.1 to 1.9
- gain_third: float32 [96], replicated, may hold values from 0.1 to 1.9
Outputs:
- pixels: float32 [8, 3, 16, 32, 64], P('groups', None, 'tile'), parts along dimension 0
There are 2 independent parts, one for each index of `groups`. A program takes and returns all parts, laid end to end along the dimension named above; an argument that names none is the same for every part. Nothing has to cross between parts.
All inputs are finite; a program needn't handle non-finite values.
Results may differ from a plain program's by a relative error of at most 0.0085.
Values may be sent and summed in bfloat16 or wider, within the bound.
A program may use at most 64 MiB of HBM per device.

v0:
```python
import functools

import jax
import jax.numpy as jnp
import numpy as np
from jax import lax
from jax.experimental import pallas as pl
from jax.experimental.pallas import tpu as pltpu
from jax.sharding import PartitionSpec as P

TILES_X = 8
epsilon = 1e-06
MESH = pl.DeviceIdType.MESH
DIRS = ((1, 0), (-1, 0), (1, 1), (1, -1), (-1, 1), (-1, -1), (0, 1), (0, -1))
BF = jnp.bfloat16
F32 = jnp.float32
NT = (((1,), (1,)), ((), ()))


def position(count):
    placed = lax.rem(lax.axis_index("tile") + TILES_X // 2, count)
    return placed // TILES_X, lax.rem(placed, TILES_X)


def inside(count, row, col):
    rows = count // TILES_X
    return (row >= 0) & (row < rows) & (col >= 0) & (col < TILES_X)


def exchange_kernel(count, rims, *refs):
    n = len(rims)
    xs, tbs, lrs, cns = refs[:n], refs[n : 2 * n], refs[2 * n : 3 * n], refs[3 * n : 4 * n]
    stages, (send_sem, recv_sem) = refs[4 * n : 5 * n], refs[5 * n :]
    me = lax.axis_index("tile")
    row, col = position(count)
    barrier = pltpu.get_barrier_semaphore()
    targets = [lax.rem(me + dr * TILES_X + dc + 2 * count, count) for dr, dc in DIRS]
    for target in targets:
        pl.semaphore_signal(barrier, inc=1, device_id={"tile": target}, device_id_type=MESH)
    for x, stage in zip(xs, stages):
        width = x.shape[2]
        stage[0] = x[:, :, 0:2, :]
        stage[1] = x[:, :, width - 2 : width, :]
    pl.semaphore_wait(barrier, len(DIRS))

    def copy(a, k):
        dr, dc = DIRS[k]
        h, height = rims[a], xs[a].shape[1]
        rows = pl.ds(height - h, h) if dr == 1 else pl.ds(0, h)
        if dc == 0:
            src, dst = xs[a].at[:, rows], tbs[a].at[0 if dr == 1 else 1]
        elif dr == 0:
            src, dst = stages[a].at[1 if dc == 1 else 0], lrs[a].at[0 if dc == 1 else 1]
        else:
            src = stages[a].at[1 if dc == 1 else 0, :, rows]
            dst = cns[a].at[(0 if dr == 1 else 2) + (0 if dc == 1 else 1)]
        return pltpu.make_async_remote_copy(
            src_ref=src,
            dst_ref=dst,
            send_sem=send_sem.at[a, k],
            recv_sem=recv_sem.at[a, k],
            device_id={"tile": targets[k]},
            device_id_type=MESH,
        )

    for a in range(n):
        for k, (dr, dc) in enumerate(DIRS):

            @pl.when(inside(count, row + dr, col + dc))
            def _():
                copy(a, k).start()

    for a in range(n):
        for k, (dr, dc) in enumerate(DIRS):

            @pl.when(inside(count, row - dr, col - dc))
            def _():
                copy(a, k).wait_recv()

            @pl.when(inside(count, row + dr, col + dc))
            def _():
                copy(a, k).wait_send()


def exchange(count, arrays, rims):
    tbs, lrs, cns, stages = [], [], [], []
    for x, h in zip(arrays, rims):
        f, height, width, c = x.shape
        tbs.append(jax.ShapeDtypeStruct((2, f, h, width, c), x.dtype))
        lrs.append(jax.ShapeDtypeStruct((2, f, height, 2, c), x.dtype))
        cns.append(jax.ShapeDtypeStruct((4, f, h, 2, c), x.dtype))
        stages.append(pltpu.VMEM((2, f, height, 2, c), x.dtype))
    n = len(arrays)
    outs = pl.pallas_call(
        functools.partial(exchange_kernel, count, rims),
        out_shape=tbs + lrs + cns,
        in_specs=[pl.BlockSpec(memory_space=pltpu.VMEM)] * n,
        out_specs=[pl.BlockSpec(memory_space=pltpu.VMEM)] * (3 * n),
        scratch_shapes=stages + [pltpu.SemaphoreType.DMA((n, len(DIRS))), pltpu.SemaphoreType.DMA((n, len(DIRS)))],
        compiler_params=pltpu.CompilerParams(collective_id=0, has_side_effects=True),
        name="exchange",
    )(*arrays)
    return outs[:n], outs[n : 2 * n], outs[2 * n :]


def activate(widened, gain, channels):
    meansq = jnp.sum(widened * widened, axis=-1, keepdims=True) * (1.0 / channels)
    normed = widened * lax.rsqrt(meansq + epsilon) * gain
    return normed / (1.0 + jnp.exp(-normed))


def decode_kernel(count, *refs):
    xs = refs[0:4]
    tbs, lrs, cns = refs[4:8], refs[8:12], refs[12:16]
    w1, w2, w3, g1, g2, g3, up2, up3, out = refs[16:25]
    p1, a1, w1s, y1, p2, a2, y2, p3, dlo, dhi, sems = refs[25:]
    frames, h1, wd1, c1 = xs[0].shape
    _, h2, wd2, c2 = xs[2].shape
    _, h3, wd3, c3 = xs[3].shape
    m1 = a1.shape[1] // (h1 + 4)
    m2 = a2.shape[2] // (h2 + 4)
    copies = []
    for t in range(3):
        for b in range(3):
            for c in range(3):
                cp = pltpu.make_async_copy(w1.at[t, b, c], w1s.at[t * 3 + b, :, pl.ds(c * c1, c1)], sems.at[t, b, c])
                cp.start()
                copies.append(cp)
    row, col = position(count)
    up_ok, down_ok = row > 0, row < count // TILES_X - 1
    left_ok, right_ok = col > 0, col < TILES_X - 1

    def kept(ok, values):
        return jnp.where(ok, values, jnp.zeros_like(values))

    def place(p, at, x, tb, lr, cn, h):
        f, height, width, c = x.shape
        fs = pl.ds(at, f)
        cs = pl.ds(0, c)
        mid, lo, hi = pl.ds(h, height), pl.ds(0, h), pl.ds(h + height, h)
        inner, left, right = pl.ds(16, width), pl.ds(14, 2), pl.ds(16 + width, 2)
        p[fs, mid, inner, cs] = x[...]
        p[fs, lo, inner, cs] = kept(up_ok, tb[0])
        p[fs, hi, inner, cs] = kept(down_ok, tb[1])
        p[fs, mid, left, cs] = kept(left_ok, lr[0])
        p[fs, mid, right, cs] = kept(right_ok, lr[1])
        p[fs, lo, left, cs] = kept(up_ok & left_ok, cn[0])
        p[fs, lo, right, cs] = kept(up_ok & right_ok, cn[1])
        p[fs, hi, left, cs] = kept(down_ok & left_ok, cn[2])
        p[fs, hi, right, cs] = kept(down_ok & right_ok, cn[3])

    place(p1, 2, xs[0], tbs[0], lrs[0], cns[0], 2)
    place(p1, 0, xs[1], tbs[1], lrs[1], cns[1], 2)
    place(p2, 0, xs[2], tbs[2], lrs[2], cns[2], 2)
    place(p3, 0, xs[3], tbs[3], lrs[3], cns[3], 1)

    gain1 = g1[...]

    @pl.loop(0, frames)
    def _(f):
        for r in range(h1 + 4):
            value = p1[f + 2, r].astype(F32)
            p1[f + 2, r] = activate(value, gain1, c1).astype(BF)

    @pl.loop(0, frames + 2)
    def _(f):
        for c in range(3):
            for r in range(h1 + 4):
                a1[f, pl.ds(r * m1, m1), pl.ds(c * c1, c1)] = p1[f, r, pl.ds(14 + c, m1), :]

    for cp in copies:
        cp.wait()

    def keep_mask(rows, pitch, used):
        flat = lax.broadcasted_iota(jnp.int32, (rows * pitch, 1), 0)
        r, c = flat // pitch, lax.rem(flat, pitch)
        return r, c, used

    gain2 = g2[...]
    o1 = h1 + 2
    flat = lax.broadcasted_iota(jnp.int32, (o1 * m1, 1), 0)
    r1, q1 = flat // m1, lax.rem(flat, m1)

    def valid(r, q, rows, cols):
        top = jnp.where(up_ok, 0, 1)
        bottom = jnp.where(down_ok, rows, rows - 1)
        first = jnp.where(left_ok, 0, 1)
        last = jnp.where(right_ok, cols, cols - 1)
        return (r >= top) & (r < bottom) & (q >= first) & (q < last)

    ok1 = valid(r1, q1, o1, wd1 + 2)

    @pl.loop(0, frames)
    def _(f):
        total = jnp.zeros((o1 * m1, c2), F32)
        for t in range(3):
            for b in range(3):
                total = total + lax.dot_general(
                    a1[f + t, pl.ds(b * m1, o1 * m1), :], w1s[t * 3 + b], NT, preferred_element_type=F32
                )
        rounded = total.astype(BF).astype(F32)
        acted = jnp.where(ok1, activate(rounded, gain2, c2), 0.0).astype(BF)
        for r in range(o1):
            y1[f, :, pl.ds(r * 256, c2)] = acted[r * m1 : (r + 1) * m1]

    pitch = h2 + 4

    @pl.loop(0, 2)
    def _(f):
        for c in range(3):
            for r in range(pitch):
                a2[f, c, pl.ds(r * m2, m2), :] = p2[f, r, pl.ds(14 + c, m2), :]

    @pl.loop(0, frames)
    def _(f):
        for r in range(o1):
            wide = jnp.dot(up2[...], y1[f, :, pl.ds(r * 256, c2)], preferred_element_type=F32).astype(BF)
            for c in range(3):
                a2[f + 2, c, pl.ds(2 * r * m2, m2), :] = wide[c * m2 : (c + 1) * m2]
                a2[f + 2, c, pl.ds((2 * r + 1) * m2, m2), :] = wide[c * m2 : (c + 1) * m2]

    gain3 = g3[...]
    o2 = h2 + 2
    chunks = 3
    per = o2 // chunks
    flat2 = lax.broadcasted_iota(jnp.int32, (per * m2, 1), 0)
    r2, q2 = flat2 // m2, lax.rem(flat2, m2)
    for f0 in range(frames):
        y2[f0] = jnp.zeros(y2.shape[1:], BF)

    @pl.loop(0, frames)
    def _(f):
        for chunk in range(chunks):
            total = jnp.zeros((per * m2, c3), F32)
            for t in range(3):
                for b in range(3):
                    for c in range(3):
                        total = total + lax.dot_general(
                            a2[f + t, c, pl.ds((chunk * per + b) * m2, per * m2), :],
                            w2[t, b, c],
                            NT,
                            preferred_element_type=F32,
                        )
            rounded = total.astype(BF).astype(F32)
            ok2 = valid(r2 + chunk * per, q2, o2, wd2 + 2)
            acted = jnp.where(ok2, activate(rounded, gain3, c3), 0.0).astype(BF)
            for r in range(per):
                y2[f, chunk * per + r, :, pl.ds(0, c3)] = acted[r * m2 : (r + 1) * m2]

    taps3 = [w3[:, pl.ds(c * 128, 128)] for c in range(3)]

    @pl.loop(0, frames)
    def _(f):
        for r in range(o2):
            wide = jnp.dot(up3[...], y2[f, r], preferred_element_type=F32).astype(BF)
            total = jnp.zeros((72, wd3), F32)
            for c in range(3):
                total = total + lax.dot_general(
                    taps3[c], wide[c * wd3 : (c + 1) * wd3], NT, preferred_element_type=F32
                )
            dlo[f, r] = total

    thin3 = [w3[:, pl.ds(c * 128, c3)] for c in range(3)]

    @pl.loop(0, h3 + 2)
    def _(r):
        for f in range(2):
            total = jnp.zeros((72, wd3), F32)
            for c in range(3):
                total = total + lax.dot_general(
                    thin3[c], p3[f, r, pl.ds(15 + c, wd3), :], NT, preferred_element_type=F32
                )
            dhi[f, r] = total

    for f in range(frames):

        @pl.loop(0, h2)
        def _(i):
            for parity in range(2):
                total = None
                for t in range(3):
                    for b in range(3):
                        part = pl.ds((t * 3 + b) * 8, 8)
                        if f + t < 2:
                            term = dhi[f + t, 2 * i + parity + b, part]
                        else:
                            term = dlo[f + t - 2, i + (parity + b + 1) // 2, part]
                        total = term if total is None else total + term
                out[f, 2 * i + parity] = total


def decode(count, arrays, tbs, lrs, cns, w1, w2, w3, g1, g2, g3):
    frames, h1, wd1, c1 = arrays[0].shape
    _, h2, wd2, c2 = arrays[2].shape
    _, h3, wd3, c3 = arrays[3].shape
    m1 = -(-(wd1 + 2) // 16) * 16
    m2 = -(-(wd2 + 2) // 16) * 16
    up2 = np.zeros((3, m2, m1), np.float32)
    up3 = np.zeros((3, wd3, m2), np.float32)
    for c in range(3):
        for q in range(wd2 + 2):
            up2[c, q, (q - 1 + c - 1) // 2 + 1] = 1
        for q in range(wd3):
            up3[c, q, (q + c - 1) // 2 + 1] = 1
    up2 = jnp.asarray(up2.reshape(3 * m2, m1), BF)
    up3 = jnp.asarray(up3.reshape(3 * wd3, m2), BF)
    rgb = w3.shape[3]
    w3 = jnp.pad(w3.transpose(0, 1, 3, 2, 4), ((0, 0), (0, 0), (0, 8 - rgb), (0, 0), (0, 128 - c3))).reshape(72, 384)
    vm = pl.BlockSpec(memory_space=pltpu.VMEM)
    hbm = pl.BlockSpec(memory_space=pl.ANY)
    scratch = [
        pltpu.VMEM((frames + 2, h1 + 4, wd1 + 32, c1), BF),
        pltpu.VMEM((frames + 2, (h1 + 4) * m1, 3 * c1), BF),
        pltpu.VMEM((9, c2, 3 * c1), BF),
        pltpu.VMEM((frames, m1, (h1 + 2) * 256), BF),
        pltpu.VMEM((2, h2 + 4, wd2 + 32, c2), BF),
        pltpu.VMEM((frames + 2, 3, (h2 + 4) * m2, c2), BF),
        pltpu.VMEM((frames, h2 + 2, m2, 128), BF),
        pltpu.VMEM((2, h3 + 2, wd3 + 32, c3), BF),
        pltpu.VMEM((frames, h2 + 2, 72, wd3), F32),
        pltpu.VMEM((2, h3 + 2, 72, wd3), F32),
        pltpu.SemaphoreType.DMA((3, 3, 3)),
    ]
    out = pl.pallas_call(
        functools.partial(decode_kernel, count),
        out_shape=jax.ShapeDtypeStruct((frames, h3, 8, wd3), F32),
        in_specs=[vm] * 16 + [hbm] + [vm] * 7,
        out_specs=vm,
        scratch_shapes=scratch,
        compiler_params=pltpu.CompilerParams(vmem_limit_bytes=60 * 1024 * 1024),
        name="decode",
    )(*arrays, *tbs, *lrs, *cns, w1, w2, w3, g1[None], g2[None], g3[None], up2, up3)
    return out[:, :, :rgb].transpose(0, 2, 1, 3)


def solution(mesh):
    count = mesh.shape["tile"]

    def body(features, cache_first, cache_second, cache_third, w1, w2, w3, g1, g2, g3):
        arrays = [x[:, :, 0].transpose(0, 2, 3, 1) for x in (features, cache_first, cache_second, cache_third)]
        tbs, lrs, cns = exchange(count, arrays, (2, 2, 2, 1))
        return decode(count, arrays, tbs, lrs, cns, w1, w2, w3, g1, g2, g3)[:, :, None]

    tiled = P("groups", None, "tile", None, None)
    return jax.shard_map(
        body,
        mesh=mesh,
        in_specs=(tiled,) * 4 + (P(),) * 6,
        out_specs=tiled,
        check_vma=False,
    )
```

profile of v0, /device:TPU:0, one launch (start us, length us, event | category | flops | bytes accessed | tf_op | source)
XLA Modules:
  0.0 75.2 jit_solution(5115197905125562463)
XLA Ops:
  0.0 1.3 %broadcast_in_dim.12.refs_19_ = f32[1,384]{1,0:T(1,128)} reshape(f32[384]{0:T(512)} %param.19) | data formatting | bytes 3072 | tf_op jit(solution)/shard_map/broadcast_in_dim | solution.py:332
  1.3 1.4 %pad.4 = bf16[3,3,8,3,128]{4,2,3,1,0:T(8,128)(2,1)} pad(bf16[3,3,3,3,96]{4,2,3,1,0:T(4,128)(2,1)} %bitcast.29, bf16[]{:T(256)} %constant.6.clone.1), padding=0_0x0_0x0_5x0_0x0_32 | pad | bytes 70850 | tf_op jit(solution)/shard_map/jit(_pad)/pad | solution.py:308
  2.6 22.9 %exchange.1 = (bf16[2,4,2,16,384]{4,3,2,1,0:T(8,128)(2,1)}, bf16[2,2,2,16,384]{4,3,2,1,0:T(8,128)(2,1)}, bf16[2,2,2,32,192]{4,3,2,1,0:T(8,128)(2,1)}, bf16[2,2,1...) custom-call(bf16[4,8,16,384]{3,2,1,0:T(8,128)(2,1)} %bitcast.24, ...), custom_call_target="tpu_custom_call" | custom-call | tf_op jit(solution)/shard_map/exchange/pallas_call | solution.py:94
  25.5 47.9 %decode.1 = f32[4,32,8,64]{3,2,1,0:T(8,128)} custom-call(bf16[4,8,16,384]{3,2,1,0:T(8,128)(2,1)} %bitcast.25, bf16[2,8,16,384]{3,2,1,0:T(8,128)(2,1)} %bitcast.27, bf16[2,16,32,192]{3,2,1,0:T(8,128)(2,1)} %bitcast.23, bf16[2,32,64,96]{3,2,1,0:T(8,128)(2,1)} %bitcast.21, bf16[2,4,2,16,384]{4,3,2,1,0:T(8,128)(2,1)} %get-tuple-element.17.refs_4_, ...), custom_call_target="tpu_custom_call" | custom-call | tf_op jit(solution)/shard_map/decode/pallas_call | solution.py:324
  73.4 1.1 %slice_bitcast_fusion = f32[4,3,1,32,64]{4,1,3,0,2:T(4,128)S(1)} fusion(f32[4,32,8,64]{3,2,1,0:T(8,128)} %decode.1), kind=kLoop, calls=%fused_computation | loop fusion | bytes 196608 | tf_op jit(solution)/shard_map/broadcast_in_dim | solution.py:342
  74.5 0.7 copy.13
where the time goes:
time: 75.5 us; the launch traced here: 75.2 us
  Pallas kernels  70.7 us (94%)
  local copies, waits for them, and re-layouts  4.41 us (6%)
    pallas_call x1, Pallas kernels, decode(): pl.pallas_call(functools.partial(decode_kernel, count), out_shape=jax.Sha...  47.9 us
    pallas_call x1, Pallas kernels, exchange(): pl.pallas_call(functools.partial(exchange_kernel, count, rims), out_shape...  22.9 us
    broadcast_in_dim x2, local copies, waits for them, and re-layouts, body(): decode(count, arrays, tbs, lrs, cns, w1, w2, w3, g1, g2, g3)[:, :, None]  1.77 us

commit v1 on v0

--- a/solution.py
+++ b/solution.py
@@ -27,10 +27,7 @@
     return (row >= 0) & (row < rows) & (col >= 0) & (col < TILES_X)
 
 
-def exchange_kernel(count, rims, *refs):
-    n = len(rims)
-    xs, tbs, lrs, cns = refs[:n], refs[n : 2 * n], refs[2 * n : 3 * n], refs[3 * n : 4 * n]
-    stages, (send_sem, recv_sem) = refs[4 * n : 5 * n], refs[5 * n :]
+def exchange_plan(count, rims, xs, tbs, lrs, cns, stages, send_sem, recv_sem):
     me = lax.axis_index("tile")
     row, col = position(count)
     barrier = pltpu.get_barrier_semaphore()
@@ -63,44 +60,28 @@
             device_id_type=MESH,
         )
 
-    for a in range(n):
+    def send(a):
         for k, (dr, dc) in enumerate(DIRS):
 
             @pl.when(inside(count, row + dr, col + dc))
             def _():
                 copy(a, k).start()
 
-    for a in range(n):
+    def receive(a):
         for k, (dr, dc) in enumerate(DIRS):
 
             @pl.when(inside(count, row - dr, col - dc))
             def _():
                 copy(a, k).wait_recv()
 
+    def finish(a):
+        for k, (dr, dc) in enumerate(DIRS):
+
             @pl.when(inside(count, row + dr, col + dc))
             def _():
                 copy(a, k).wait_send()
 
-
-def exchange(count, arrays, rims):
-    tbs, lrs, cns, stages = [], [], [], []
-    for x, h in zip(arrays, rims):
-        f, height, width, c = x.shape
-        tbs.append(jax.ShapeDtypeStruct((2, f, h, width, c), x.dtype))
-        lrs.append(jax.ShapeDtypeStruct((2, f, height, 2, c), x.dtype))
-        cns.append(jax.ShapeDtypeStruct((4, f, h, 2, c), x.dtype))
-        stages.append(pltpu.VMEM((2, f, height, 2, c), x.dtype))
-    n = len(arrays)
-    outs = pl.pallas_call(
-        functools.partial(exchange_kernel, count, rims),
-        out_shape=tbs + lrs + cns,
-        in_specs=[pl.BlockSpec(memory_space=pltpu.VMEM)] * n,
-        out_specs=[pl.BlockSpec(memory_space=pltpu.VMEM)] * (3 * n),
-        scratch_shapes=stages + [pltpu.SemaphoreType.DMA((n, len(DIRS))), pltpu.SemaphoreType.DMA((n, len(DIRS)))],
-        compiler_params=pltpu.CompilerParams(collective_id=0, has_side_effects=True),
-        name="exchange",
-    )(*arrays)
-    return outs[:n], outs[n : 2 * n], outs[2 * n :]
+    return send, receive, finish
 
 
 def activate(widened, gain, channels):
@@ -109,11 +90,11 @@
     return normed / (1.0 + jnp.exp(-normed))
 
 
-def decode_kernel(count, *refs):
+def decode_kernel(count, rims, *refs):
     xs = refs[0:4]
-    tbs, lrs, cns = refs[4:8], refs[8:12], refs[12:16]
-    w1, w2, w3, g1, g2, g3, up2, up3, out = refs[16:25]
-    p1, a1, w1s, y1, p2, a2, y2, p3, dlo, dhi, sems = refs[25:]
+    w1, w2, w3, g1, g2, g3, up2, up3, out = refs[4:13]
+    tbs, lrs, cns, stages = refs[13:17], refs[17:21], refs[21:25], refs[25:29]
+    p1, a1, w1s, w2s, y1, p2, a2, y2, p3, dlo, dhi, sems, send_sem, recv_sem = refs[29:]
     frames, h1, wd1, c1 = xs[0].shape
     _, h2, wd2, c2 = xs[2].shape
     _, h3, wd3, c3 = xs[3].shape
@@ -126,6 +107,11 @@
                 cp = pltpu.make_async_copy(w1.at[t, b, c], w1s.at[t * 3 + b, :, pl.ds(c * c1, c1)], sems.at[t, b, c])
                 cp.start()
                 copies.append(cp)
+    second = pltpu.make_async_copy(w2, w2s, sems.at[3, 0, 0])
+    second.start()
+    send, receive, finish = exchange_plan(count, rims, xs, tbs, lrs, cns, stages, send_sem, recv_sem)
+    for a in (3, 0, 1, 2):
+        send(a)
     row, col = position(count)
     up_ok, down_ok = row > 0, row < count // TILES_X - 1
     left_ok, right_ok = col > 0, col < TILES_X - 1
@@ -149,10 +135,24 @@
         p[fs, hi, left, cs] = kept(down_ok & left_ok, cn[2])
         p[fs, hi, right, cs] = kept(down_ok & right_ok, cn[3])
 
+    receive(3)
+    place(p3, 0, xs[3], tbs[3], lrs[3], cns[3], 1)
+    thin3 = [w3[:, pl.ds(c * 128, c3)] for c in range(3)]
+
+    @pl.loop(0, h3 + 2)
+    def _(r):
+        for f in range(2):
+            total = jnp.zeros((72, wd3), F32)
+            for c in range(3):
+                total = total + lax.dot_general(
+                    thin3[c], p3[f, r, pl.ds(15 + c, wd3), :], NT, preferred_element_type=F32
+                )
+            dhi[f, r] = total
+
+    receive(0)
     place(p1, 2, xs[0], tbs[0], lrs[0], cns[0], 2)
+    receive(1)
     place(p1, 0, xs[1], tbs[1], lrs[1], cns[1], 2)
-    place(p2, 0, xs[2], tbs[2], lrs[2], cns[2], 2)
-    place(p3, 0, xs[3], tbs[3], lrs[3], cns[3], 1)
 
     gain1 = g1[...]
 
@@ -170,11 +170,6 @@
 
     for cp in copies:
         cp.wait()
-
-    def keep_mask(rows, pitch, used):
-        flat = lax.broadcasted_iota(jnp.int32, (rows * pitch, 1), 0)
-        r, c = flat // pitch, lax.rem(flat, pitch)
-        return r, c, used
 
     gain2 = g2[...]
     o1 = h1 + 2
@@ -203,6 +198,8 @@
         for r in range(o1):
             y1[f, :, pl.ds(r * 256, c2)] = acted[r * m1 : (r + 1) * m1]
 
+    receive(2)
+    place(p2, 0, xs[2], tbs[2], lrs[2], cns[2], 2)
     pitch = h2 + 4
 
     @pl.loop(0, 2)
@@ -219,6 +216,7 @@
                 a2[f + 2, c, pl.ds(2 * r * m2, m2), :] = wide[c * m2 : (c + 1) * m2]
                 a2[f + 2, c, pl.ds((2 * r + 1) * m2, m2), :] = wide[c * m2 : (c + 1) * m2]
 
+    second.wait()
     gain3 = g3[...]
     o2 = h2 + 2
     chunks = 3
@@ -237,7 +235,7 @@
                     for c in range(3):
                         total = total + lax.dot_general(
                             a2[f + t, c, pl.ds((chunk * per + b) * m2, per * m2), :],
-                            w2[t, b, c],
+                            w2s[t, b, c],
                             NT,
                             preferred_element_type=F32,
                         )
@@ -259,18 +257,6 @@
                     taps3[c], wide[c * wd3 : (c + 1) * wd3], NT, preferred_element_type=F32
                 )
             dlo[f, r] = total
-
-    thin3 = [w3[:, pl.ds(c * 128, c3)] for c in range(3)]
-
-    @pl.loop(0, h3 + 2)
-    def _(r):
-        for f in range(2):
-            total = jnp.zeros((72, wd3), F32)
-            for c in range(3):
-                total = total + lax.dot_general(
-                    thin3[c], p3[f, r, pl.ds(15 + c, wd3), :], NT, preferred_element_type=F32
-                )
-            dhi[f, r] = total
 
     for f in range(frames):
 
@@ -288,8 +274,11 @@
                         total = term if total is None else total + term
                 out[f, 2 * i + parity] = total
 
-
-def decode(count, arrays, tbs, lrs, cns, w1, w2, w3, g1, g2, g3):
+    for a in range(4):
+        finish(a)
+
+
+def decode(count, rims, arrays, w1, w2, w3, g1, g2, g3):
     frames, h1, wd1, c1 = arrays[0].shape
     _, h2, wd2, c2 = arrays[2].shape
     _, h3, wd3, c3 = arrays[3].shape
@@ -308,10 +297,18 @@
     w3 = jnp.pad(w3.transpose(0, 1, 3, 2, 4), ((0, 0), (0, 0), (0, 8 - rgb), (0, 0), (0, 128 - c3))).reshape(72, 384)
     vm = pl.BlockSpec(memory_space=pltpu.VMEM)
     hbm = pl.BlockSpec(memory_space=pl.ANY)
-    scratch = [
+    tbs, lrs, cns, stages = [], [], [], []
+    for x, h in zip(arrays, rims):
+        f, height, width, c = x.shape
+        tbs.append(pltpu.VMEM((2, f, h, width, c), BF))
+        lrs.append(pltpu.VMEM((2, f, height, 2, c), BF))
+        cns.append(pltpu.VMEM((4, f, h, 2, c), BF))
+        stages.append(pltpu.VMEM((2, f, height, 2, c), BF))
+    scratch = tbs + lrs + cns + stages + [
         pltpu.VMEM((frames + 2, h1 + 4, wd1 + 32, c1), BF),
         pltpu.VMEM((frames + 2, (h1 + 4) * m1, 3 * c1), BF),
         pltpu.VMEM((9, c2, 3 * c1), BF),
+        pltpu.VMEM(w2.shape, BF),
         pltpu.VMEM((frames, m1, (h1 + 2) * 256), BF),
         pltpu.VMEM((2, h2 + 4, wd2 + 32, c2), BF),
         pltpu.VMEM((frames + 2, 3, (h2 + 4) * m2, c2), BF),
@@ -319,17 +316,21 @@
         pltpu.VMEM((2, h3 + 2, wd3 + 32, c3), BF),
         pltpu.VMEM((frames, h2 + 2, 72, wd3), F32),
         pltpu.VMEM((2, h3 + 2, 72, wd3), F32),
-        pltpu.SemaphoreType.DMA((3, 3, 3)),
+        pltpu.SemaphoreType.DMA((4, 3, 3)),
+        pltpu.SemaphoreType.DMA((4, len(DIRS))),
+        pltpu.SemaphoreType.DMA((4, len(DIRS))),
     ]
     out = pl.pallas_call(
-        functools.partial(decode_kernel, count),
+        functools.partial(decode_kernel, count, rims),
         out_shape=jax.ShapeDtypeStruct((frames, h3, 8, wd3), F32),
-        in_specs=[vm] * 16 + [hbm] + [vm] * 7,
+        in_specs=[vm] * 4 + [hbm] * 2 + [vm] * 6,
         out_specs=vm,
         scratch_shapes=scratch,
-        compiler_params=pltpu.CompilerParams(vmem_limit_bytes=60 * 1024 * 1024),
+        compiler_params=pltpu.CompilerParams(
+            collective_id=0, has_side_effects=True, vmem_limit_bytes=60 * 1024 * 1024
+        ),
         name="decode",
-    )(*arrays, *tbs, *lrs, *cns, w1, w2, w3, g1[None], g2[None], g3[None], up2, up3)
+    )(*arrays, w1, w2, w3, g1[None], g2[None], g3[None], up2, up3)
     return out[:, :, :rgb].transpose(0, 2, 1, 3)
 
 
@@ -338,8 +339,7 @@
 
     def body(features, cache_first, cache_second, cache_third, w1, w2, w3, g1, g2, g3):
         arrays = [x[:, :, 0].transpose(0, 2, 3, 1) for x in (features, cache_first, cache_second, cache_third)]
-        tbs, lrs, cns = exchange(count, arrays, (2, 2, 2, 1))
-        return decode(count, arrays, tbs, lrs, cns, w1, w2, w3, g1, g2, g3)[:, :, None]
+        return decode(count, (2, 2, 2, 1), arrays, w1, w2, w3, g1, g2, g3)[:, :, None]
 
     tiled = P("groups", None, "tile", None, None)
     return jax.shard_map(

time: 75.5 us -> 67 us (0.89)
  Pallas kernels: 70.7 us -> 62.3 us
    pallas_call x2 -> x1, Pallas kernels: 70.7 us -> 62.3 us  [decode(): pl.pallas_call(functools.partial(decode_kernel, count, rims), out_shape=j...]
where the time goes in v1:
time: 67 us; the launch traced here: 66.7 us
  Pallas kernels  62.3 us (93%)
  local copies, waits for them, and re-layouts  4.43 us (7%)
    pallas_call x1, Pallas kernels, decode(): pl.pallas_call(functools.partial(decode_kernel, count, rims), out_shape=j...  62.3 us
    broadcast_in_dim x2, local copies, waits for them, and re-layouts, body(): decode(count, (2, 2, 2, 1), arrays, w1, w2, w3, g1, g2, g3)[:, :, None]  1.77 us
    pad x1, local copies, waits for them, and re-layouts, decode(): jnp.pad(w3.transpose(0, 1, 3, 2, 4), ((0, 0), (0, 0), (0, 8 - rgb), (0, 0...  1.38 us

profile of v1, /device:TPU:0, one launch (start us, length us, event | category | flops | bytes accessed | tf_op | source)
XLA Modules:
  0.0 66.7 jit_solution(2781724521406875940)
XLA Ops:
  0.0 1.3 %broadcast_in_dim.12.refs_7_ = f32[1,384]{1,0:T(1,128)} reshape(f32[384]{0:T(512)} %param.19) | data formatting | bytes 3072 | tf_op jit(solution)/shard_map/broadcast_in_dim | solution.py:333
  1.3 1.4 %pad.4 = bf16[3,3,8,3,128]{4,2,3,1,0:T(8,128)(2,1)} pad(bf16[3,3,3,3,96]{4,2,3,1,0:T(4,128)(2,1)} %bitcast.25, bf16[]{:T(256)} %constant.6.clone.1), padding=0_0x0_0x0_5x0_0x0_32 | pad | bytes 70850 | tf_op jit(solution)/shard_map/jit(_pad)/pad | solution.py:297
  2.7 62.3 %decode.1 = f32[4,32,8,64]{3,2,1,0:T(8,128)} custom-call(bf16[4,8,16,384]{3,2,1,0:T(8,128)(2,1)} %bitcast.22, bf16[2,8,16,384]{3,2,1,0:T(8,128)(2,1)} %bitcast.24, bf16[2,16,32,192]{3,2,1,0:T(8,128)(2,1)} %bitcast.21, bf16[2,32,64,96]{3,2,1,0:T(8,128)(2,1)} %bitcast.20, bf16[3,3,3,192,384]{4,3,2,1,0:T(8,128)(2,1)} %refs_4_.1, ...), custom_call_target="tpu_custom_call" | custom-call | tf_op jit(solution)/shard_map/decode/pallas_call | solution.py:323
  65.0 1.1 %slice_bitcast_fusion = f32[4,3,1,32,64]{4,1,3,0,2:T(4,128)S(1)} fusion(f32[4,32,8,64]{3,2,1,0:T(8,128)} %decode.1), kind=kLoop, calls=%fused_computation | loop fusion | bytes 196608 | tf_op jit(solution)/shard_map/broadcast_in_dim | solution.py:342
  66.0 0.7 %copy.13 = f32[4,3,1,32,64]{4,3,2,1,0:T(8,128)} copy(f32[4,3,1,32,64]{4,1,3,0,2:T(4,128)S(1)} %slice_bitcast_fusion) | data formatting | bytes 196608 | tf_op jit(solution)/shard_map/broadcast_in_dim | solution.py:342

commit v2 on v1

--- a/solution.py
+++ b/solution.py
@@ -94,7 +94,7 @@
     xs = refs[0:4]
     w1, w2, w3, g1, g2, g3, up2, up3, out = refs[4:13]
     tbs, lrs, cns, stages = refs[13:17], refs[17:21], refs[21:25], refs[25:29]
-    p1, a1, w1s, w2s, y1, p2, a2, y2, p3, dlo, dhi, sems, send_sem, recv_sem = refs[29:]
+    p1, a1, w1s, w2s, w2p, wlo, y1, p2, a2, y2, p3, dlo, dhi, sems, send_sem, recv_sem = refs[29:]
     frames, h1, wd1, c1 = xs[0].shape
     _, h2, wd2, c2 = xs[2].shape
     _, h3, wd3, c3 = xs[3].shape
@@ -135,19 +135,25 @@
         p[fs, hi, left, cs] = kept(down_ok & left_ok, cn[2])
         p[fs, hi, right, cs] = kept(down_ok & right_ok, cn[3])
 
+    w2p[...] = jnp.zeros(w2p.shape, BF)
+    second.wait()
+    for t in range(3):
+        for c in range(3):
+            for b in range(3):
+                w2p[t * 3 + c, pl.ds(b * 128, c3)] = w2s[t, b, c]
     receive(3)
     place(p3, 0, xs[3], tbs[3], lrs[3], cns[3], 1)
     thin3 = [w3[:, pl.ds(c * 128, c3)] for c in range(3)]
 
-    @pl.loop(0, h3 + 2)
-    def _(r):
+    @pl.loop(0, (h3 + 2) // 2)
+    def _(i):
         for f in range(2):
-            total = jnp.zeros((72, wd3), F32)
-            for c in range(3):
-                total = total + lax.dot_general(
-                    thin3[c], p3[f, r, pl.ds(15 + c, wd3), :], NT, preferred_element_type=F32
-                )
-            dhi[f, r] = total
+            total = jnp.zeros((2 * wd3, 128), F32)
+            for c in range(3):
+                window = p3[f, pl.ds(2 * i, 2), pl.ds(15 + c, wd3), :].reshape(2 * wd3, c3)
+                total = total + lax.dot_general(window, thin3[c], NT, preferred_element_type=F32)
+            for r in range(2):
+                dhi[f, 2 * i + r] = total[r * wd3 : (r + 1) * wd3].T[:72]
 
     receive(0)
     place(p1, 2, xs[0], tbs[0], lrs[0], cns[0], 2)
@@ -216,7 +222,6 @@
                 a2[f + 2, c, pl.ds(2 * r * m2, m2), :] = wide[c * m2 : (c + 1) * m2]
                 a2[f + 2, c, pl.ds((2 * r + 1) * m2, m2), :] = wide[c * m2 : (c + 1) * m2]
 
-    second.wait()
     gain3 = g3[...]
     o2 = h2 + 2
     chunks = 3
@@ -229,17 +234,26 @@
     @pl.loop(0, frames)
     def _(f):
         for chunk in range(chunks):
-            total = jnp.zeros((per * m2, c3), F32)
+            pair = jnp.zeros(((per + 1) * m2, 256), F32)
+            single = jnp.zeros((per * m2, 128), F32)
             for t in range(3):
-                for b in range(3):
-                    for c in range(3):
-                        total = total + lax.dot_general(
-                            a2[f + t, c, pl.ds((chunk * per + b) * m2, per * m2), :],
-                            w2s[t, b, c],
-                            NT,
-                            preferred_element_type=F32,
-                        )
-            rounded = total.astype(BF).astype(F32)
+                for c in range(3):
+                    pair = pair + lax.dot_general(
+                        a2[f + t, c, pl.ds(chunk * per * m2, (per + 1) * m2), :],
+                        w2p[t * 3 + c, pl.ds(0, 256)],
+                        NT,
+                        preferred_element_type=F32,
+                    )
+            for t in range(3):
+                for c in range(3):
+                    single = single + lax.dot_general(
+                        a2[f + t, c, pl.ds((chunk * per + 2) * m2, per * m2), :],
+                        w2p[t * 3 + c, pl.ds(256, 128)],
+                        NT,
+                        preferred_element_type=F32,
+                    )
+            total = pair[: per * m2, :128] + pair[m2:, 128:] + single
+            rounded = total.astype(BF).astype(F32)[:, :c3]
             ok2 = valid(r2 + chunk * per, q2, o2, wd2 + 2)
             acted = jnp.where(ok2, activate(rounded, gain3, c3), 0.0).astype(BF)
             for r in range(per):
@@ -251,12 +265,16 @@
     def _(f):
         for r in range(o2):
             wide = jnp.dot(up3[...], y2[f, r], preferred_element_type=F32).astype(BF)
-            total = jnp.zeros((72, wd3), F32)
+            for c in range(3):
+                wlo[c, pl.ds(r * wd3, wd3), :] = wide[c * wd3 : (c + 1) * wd3]
+        for chunk in range(chunks):
+            total = jnp.zeros((per * wd3, 128), F32)
             for c in range(3):
                 total = total + lax.dot_general(
-                    taps3[c], wide[c * wd3 : (c + 1) * wd3], NT, preferred_element_type=F32
+                    wlo[c, pl.ds(chunk * per * wd3, per * wd3), :], taps3[c], NT, preferred_element_type=F32
                 )
-            dlo[f, r] = total
+            for r in range(per):
+                dlo[f, chunk * per + r] = total[r * wd3 : (r + 1) * wd3].T[:72]
 
     for f in range(frames):
 
@@ -295,6 +313,7 @@
     up3 = jnp.asarray(up3.reshape(3 * wd3, m2), BF)
     rgb = w3.shape[3]
     w3 = jnp.pad(w3.transpose(0, 1, 3, 2, 4), ((0, 0), (0, 0), (0, 8 - rgb), (0, 0), (0, 128 - c3))).reshape(72, 384)
+    w3 = jnp.pad(w3, ((0, 56), (0, 0)))
     vm = pl.BlockSpec(memory_space=pltpu.VMEM)
     hbm = pl.BlockSpec(memory_space=pl.ANY)
     tbs, lrs, cns, stages = [], [], [], []
@@ -309,6 +328,8 @@
         pltpu.VMEM((frames + 2, (h1 + 4) * m1, 3 * c1), BF),
         pltpu.VMEM((9, c2, 3 * c1), BF),
         pltpu.VMEM(w2.shape, BF),
+        pltpu.VMEM((9, 384, c2), BF),
+        pltpu.VMEM((3, (h2 + 2) * wd3, 128), BF),
         pltpu.VMEM((frames, m1, (h1 + 2) * 256), BF),
         pltpu.VMEM((2, h2 + 4, wd2 + 32, c2), BF),
         pltpu.VMEM((frames + 2, 3, (h2 + 4) * m2, c2), BF),

time: 67 us -> 57.1 us (0.85)
  Pallas kernels: 62.3 us -> 52.3 us
    pallas_call x1, Pallas kernels: 62.3 us -> 52.3 us  [decode(): pl.pallas_call(functools.partial(decode_kernel, count, rims), out_shape=j...]
where the time goes in v2:
time: 57.1 us; the launch traced here: 56.8 us
  Pallas kernels  52.3 us (92%)
  local copies, waits for them, and re-layouts  4.46 us (8%)
    pallas_call x1, Pallas kernels, decode(): pl.pallas_call(functools.partial(decode_kernel, count, rims), out_shape=j...  52.3 us
    broadcast_in_dim x2, local copies, waits for them, and re-layouts, body(): decode(count, (2, 2, 2, 1), arrays, w1, w2, w3, g1, g2, g3)[:, :, None]  1.77 us
    broadcast_in_dim x1, local copies, waits for them, and re-layouts, decode(): g1[None]  1.27 us

profile of v2, /device:TPU:0, one launch (start us, length us, event | category | flops | bytes accessed | tf_op | source)
XLA Modules:
  0.0 56.8 jit_solution(9729733538485104047)
XLA Ops:
  0.0 1.3 %broadcast_in_dim.12.refs_7_ = f32[1,384]{1,0:T(1,128)} reshape(f32[384]{0:T(512)} %param.19) | data formatting | bytes 3072 | tf_op jit(solution)/shard_map/broadcast_in_dim | solution.py:354
  1.3 0.8 %pad.8 = bf16[3,3,8,3,128]{4,2,3,1,0:T(8,128)(2,1)S(1)} pad(bf16[3,3,3,3,96]{4,2,3,1,0:T(4,128)(2,1)} %bitcast.25, bf16[]{:T(256)} %constant.6.clone.1), padding=0_0x0_0x0_5x0_0x0_32 | pad | bytes 70850 | tf_op jit(solution)/shard_map/jit(_pad)/pad | solution.py:315
  2.0 0.7 %pad.9.refs_6_ = bf16[128,384]{1,0:T(8,128)(2,1)} pad(bf16[72,384]{1,0:T(8,128)(2,1)S(1)} %bitcast.23, bf16[]{:T(256)} %constant.6.clone.1), padding=0_56x0_0 | pad | bytes 153602 | tf_op jit(solution)/shard_map/jit(_pad)/pad | solution.py:316
  2.7 52.3 %decode.1 = f32[4,32,8,64]{3,2,1,0:T(8,128)} custom-call(bf16[4,8,16,384]{3,2,1,0:T(8,128)(2,1)} %bitcast.22, bf16[2,8,16,384]{3,2,1,0:T(8,128)(2,1)} %bitcast.24, bf16[2,16,32,192]{3,2,1,0:T(8,128)(2,1)} %bitcast.21, bf16[2,32,64,96]{3,2,1,0:T(8,128)(2,1)} %bitcast.20, bf16[3,3,3,192,384]{4,3,2,1,0:T(8,128)(2,1)} %refs_4_.1, ...), custom_call_target="tpu_custom_call" | custom-call | tf_op jit(solution)/shard_map/decode/pallas_call | solution.py:344
  55.0 1.1 %slice_bitcast_fusion = f32[4,3,1,32,64]{4,1,3,0,2:T(4,128)S(1)} fusion(f32[4,32,8,64]{3,2,1,0:T(8,128)} %decode.1), kind=kLoop, calls=%fused_computation | loop fusion | bytes 196608 | tf_op jit(solution)/shard_map/broadcast_in_dim | solution.py:363
  56.1 0.7 %copy.13 = f32[4,3,1,32,64]{4,3,2,1,0:T(8,128)} copy(f32[4,3,1,32,64]{4,1,3,0,2:T(4,128)S(1)} %slice_bitcast_fusion) | data formatting | bytes 196608 | tf_op jit(solution)/shard_map/broadcast_in_dim | solution.py:363

commit v3 on v2

--- a/solution.py
+++ b/solution.py
@@ -67,8 +67,10 @@
             def _():
                 copy(a, k).start()
 
-    def receive(a):
+    def receive(a, level):
         for k, (dr, dc) in enumerate(DIRS):
+            if level != abs(dr):
+                continue
 
             @pl.when(inside(count, row - dr, col - dc))
             def _():
@@ -119,17 +121,19 @@
     def kept(ok, values):
         return jnp.where(ok, values, jnp.zeros_like(values))
 
-    def place(p, at, x, tb, lr, cn, h):
+    def place(level, p, at, x, tb, lr, cn, h):
         f, height, width, c = x.shape
         fs = pl.ds(at, f)
         cs = pl.ds(0, c)
         mid, lo, hi = pl.ds(h, height), pl.ds(0, h), pl.ds(h + height, h)
         inner, left, right = pl.ds(16, width), pl.ds(14, 2), pl.ds(16 + width, 2)
-        p[fs, mid, inner, cs] = x[...]
+        if level == 0:
+            p[fs, mid, inner, cs] = x[...]
+            p[fs, mid, left, cs] = kept(left_ok, lr[0])
+            p[fs, mid, right, cs] = kept(right_ok, lr[1])
+            return
         p[fs, lo, inner, cs] = kept(up_ok, tb[0])
         p[fs, hi, inner, cs] = kept(down_ok, tb[1])
-        p[fs, mid, left, cs] = kept(left_ok, lr[0])
-        p[fs, mid, right, cs] = kept(right_ok, lr[1])
         p[fs, lo, left, cs] = kept(up_ok & left_ok, cn[0])
         p[fs, lo, right, cs] = kept(up_ok & right_ok, cn[1])
         p[fs, hi, left, cs] = kept(down_ok & left_ok, cn[2])
@@ -141,46 +145,21 @@
         for c in range(3):
             for b in range(3):
                 w2p[t * 3 + c, pl.ds(b * 128, c3)] = w2s[t, b, c]
-    receive(3)
-    place(p3, 0, xs[3], tbs[3], lrs[3], cns[3], 1)
-    thin3 = [w3[:, pl.ds(c * 128, c3)] for c in range(3)]
-
-    @pl.loop(0, (h3 + 2) // 2)
-    def _(i):
-        for f in range(2):
-            total = jnp.zeros((2 * wd3, 128), F32)
-            for c in range(3):
-                window = p3[f, pl.ds(2 * i, 2), pl.ds(15 + c, wd3), :].reshape(2 * wd3, c3)
-                total = total + lax.dot_general(window, thin3[c], NT, preferred_element_type=F32)
-            for r in range(2):
-                dhi[f, 2 * i + r] = total[r * wd3 : (r + 1) * wd3].T[:72]
-
-    receive(0)
-    place(p1, 2, xs[0], tbs[0], lrs[0], cns[0], 2)
-    receive(1)
-    place(p1, 0, xs[1], tbs[1], lrs[1], cns[1], 2)
-
-    gain1 = g1[...]
-
-    @pl.loop(0, frames)
-    def _(f):
-        for r in range(h1 + 4):
-            value = p1[f + 2, r].astype(F32)
-            p1[f + 2, r] = activate(value, gain1, c1).astype(BF)
-
-    @pl.loop(0, frames + 2)
-    def _(f):
-        for c in range(3):
-            for r in range(h1 + 4):
-                a1[f, pl.ds(r * m1, m1), pl.ds(c * c1, c1)] = p1[f, r, pl.ds(14 + c, m1), :]
-
-    for cp in copies:
-        cp.wait()
-
-    gain2 = g2[...]
+    gain1, gain2 = g1[...], g2[...]
     o1 = h1 + 2
-    flat = lax.broadcasted_iota(jnp.int32, (o1 * m1, 1), 0)
-    r1, q1 = flat // m1, lax.rem(flat, m1)
+
+    def prepare(rows):
+        @pl.loop(0, frames)
+        def _(f):
+            for r in rows:
+                value = p1[f + 2, r].astype(F32)
+                p1[f + 2, r] = activate(value, gain1, c1).astype(BF)
+
+        @pl.loop(0, frames + 2)
+        def _(f):
+            for c in range(3):
+                for r in rows:
+                    a1[f, pl.ds(r * m1, m1), pl.ds(c * c1, c1)] = p1[f, r, pl.ds(14 + c, m1), :]
 
     def valid(r, q, rows, cols):
         top = jnp.where(up_ok, 0, 1)
@@ -189,23 +168,62 @@
         last = jnp.where(right_ok, cols, cols - 1)
         return (r >= top) & (r < bottom) & (q >= first) & (q < last)
 
-    ok1 = valid(r1, q1, o1, wd1 + 2)
-
-    @pl.loop(0, frames)
-    def _(f):
-        total = jnp.zeros((o1 * m1, c2), F32)
+    def section_one(first_frame, some, start, rows):
+        size = rows * m1
+        total = jnp.zeros((some * size, c2), F32)
         for t in range(3):
             for b in range(3):
+                window = a1[pl.ds(first_frame + t, some), pl.ds((start + b) * m1, size), :]
                 total = total + lax.dot_general(
-                    a1[f + t, pl.ds(b * m1, o1 * m1), :], w1s[t * 3 + b], NT, preferred_element_type=F32
+                    window.reshape(some * size, 3 * c1), w1s[t * 3 + b], NT, preferred_element_type=F32
                 )
+        flat = lax.broadcasted_iota(jnp.int32, (some * size, 1), 0)
+        r1, q1 = lax.rem(flat // m1, rows) + start, lax.rem(flat, m1)
         rounded = total.astype(BF).astype(F32)
-        acted = jnp.where(ok1, activate(rounded, gain2, c2), 0.0).astype(BF)
-        for r in range(o1):
-            y1[f, :, pl.ds(r * 256, c2)] = acted[r * m1 : (r + 1) * m1]
-
-    receive(2)
-    place(p2, 0, xs[2], tbs[2], lrs[2], cns[2], 2)
+        acted = jnp.where(valid(r1, q1, o1, wd1 + 2), activate(rounded, gain2, c2), 0.0).astype(BF)
+        for f in range(some):
+            for r in range(rows):
+                part = acted[(f * rows + r) * m1 : (f * rows + r + 1) * m1]
+                y1[first_frame + f, :, pl.ds((start + r) * 256, c2)] = part
+
+    for a in range(2):
+        receive(a, 0)
+        place(0, p1, 2 - 2 * a, xs[a], tbs[a], lrs[a], cns[a], 2)
+    prepare(range(2, h1 + 2))
+    for cp in copies:
+        cp.wait()
+
+    @pl.loop(0, frames)
+    def _(f):
+        section_one(f, 1, 2, h1 - 2)
+
+    receive(3, 0)
+    place(0, p3, 0, xs[3], tbs[3], lrs[3], cns[3], 1)
+    receive(3, 1)
+    place(1, p3, 0, xs[3], tbs[3], lrs[3], cns[3], 1)
+    thin3 = [w3[:, pl.ds(c * 128, c3)] for c in range(3)]
+
+    @pl.loop(0, (h3 + 2) // 2)
+    def _(i):
+        for f in range(2):
+            total = jnp.zeros((2 * wd3, 128), F32)
+            for c in range(3):
+                window = p3[f, pl.ds(2 * i, 2), pl.ds(15 + c, wd3), :].reshape(2 * wd3, c3)
+                total = total + lax.dot_general(window, thin3[c], NT, preferred_element_type=F32)
+            for r in range(2):
+                dhi[f, 2 * i + r] = total[r * wd3 : (r + 1) * wd3].T[:72]
+
+    for a in range(2):
+        receive(a, 1)
+        place(1, p1, 2 - 2 * a, xs[a], tbs[a], lrs[a], cns[a], 2)
+    prepare((0, 1, h1 + 2, h1 + 3))
+    section_one(0, frames, 0, 2)
+    section_one(0, frames, h1, 2)
+
+    receive(2, 0)
+    place(0, p2, 0, xs[2], tbs[2], lrs[2], cns[2], 2)
+    receive(2, 1)
+    place(1, p2, 0, xs[2], tbs[2], lrs[2], cns[2], 2)
     pitch = h2 + 4
 
     @pl.loop(0, 2)

time: 57.1 us -> 60.5 us (1.060)
  the two profiles are of different devices: /device:TPU:0 before, /device:TPU:16 now
where the time goes in v3:
time: 60.5 us; the launch traced here: 60.3 us
  Pallas kernels  55.8 us (92%)
  local copies, waits for them, and re-layouts  4.46 us (7%)
    pallas_call x1, Pallas kernels, decode(): pl.pallas_call(functools.partial(decode_kernel, count, rims), out_shape=j...  55.8 us
    broadcast_in_dim x2, local copies, waits for them, and re-layouts, body(): decode(count, (2, 2, 2, 1), arrays, w1, w2, w3, g1, g2, g3)[:, :, None]  1.77 us
    broadcast_in_dim x1, local copies, waits for them, and re-layouts, decode(): g1[None]  1.27 us

profile of v3, /device:TPU:16, one launch (start us, length us, event | category | flops | bytes accessed | tf_op | source)
XLA Modules:
  0.0 60.3 jit_solution(3835042586223721590)
XLA Ops:
  0.0 1.3 %broadcast_in_dim.12.refs_7_ = f32[1,384]{1,0:T(1,128)} reshape(f32[384]{0:T(512)} %param.19) | data formatting | bytes 3072 | tf_op jit(solution)/shard_map/broadcast_in_dim | solution.py:372
  1.3 0.8 %pad.8 = bf16[3,3,8,3,128]{4,2,3,1,0:T(8,128)(2,1)S(1)} pad(bf16[3,3,3,3,96]{4,2,3,1,0:T(4,128)(2,1)} %bitcast.25, bf16[]{:T(256)} %constant.6.clone.1), padding=0_0x0_0x0_5x0_0x0_32 | pad | bytes 70850 | tf_op jit(solution)/shard_map/jit(_pad)/pad | solution.py:333
  2.0 0.7 %pad.9.refs_6_ = bf16[128,384]{1,0:T(8,128)(2,1)} pad(bf16[72,384]{1,0:T(8,128)(2,1)S(1)} %bitcast.23, bf16[]{:T(256)} %constant.6.clone.1), padding=0_56x0_0 | pad | bytes 153602 | tf_op jit(solution)/shard_map/jit(_pad)/pad | solution.py:334
  2.7 55.8 %decode.1 = f32[4,32,8,64]{3,2,1,0:T(8,128)} custom-call(bf16[4,8,16,384]{3,2,1,0:T(8,128)(2,1)} %bitcast.22, bf16[2,8,16,384]{3,2,1,0:T(8,128)(2,1)} %bitcast.24, bf16[2,16,32,192]{3,2,1,0:T(8,128)(2,1)} %bitcast.21, bf16[2,32,64,96]{3,2,1,0:T(8,128)(2,1)} %bitcast.20, bf16[3,3,3,192,384]{4,3,2,1,0:T(8,128)(2,1)} %refs_4_.1, ...), custom_call_target="tpu_custom_call" | custom-call | tf_op jit(solution)/shard_map/decode/pallas_call | solution.py:362
  58.5 1.1 %slice_bitcast_fusion = f32[4,3,1,32,64]{4,1,3,0,2:T(4,128)S(1)} fusion(f32[4,32,8,64]{3,2,1,0:T(8,128)} %decode.1), kind=kLoop, calls=%fused_computation | loop fusion | bytes 196608 | tf_op jit(solution)/shard_map/broadcast_in_dim | solution.py:381
  59.6 0.7 %copy.13 = f32[4,3,1,32,64]{4,3,2,1,0:T(8,128)} copy(f32[4,3,1,32,64]{4,1,3,0,2:T(4,128)S(1)} %slice_bitcast_fusion) | data formatting | bytes 196608 | tf_op jit(solution)/shard_map/broadcast_in_dim | solution.py:381
